TPU v7x, 256 devices: a whole 4x4x8 slice. The times are simulated.
256 devices in a mesh: leaf: 16 (over y, x), col: 16 (over z, core).
Axes of the slice: x: 4, y: 4, z: 8, core: 2. Of those that a mesh axis runs over, the one named last changes fastest.
Arguments:
- right_sides: bfloat16 [16, 2, 1792, 128], P('leaf', None, 'col'), may hold values from -6 to 6
- leaf_inverse: bfloat16 [16, 1792, 1792], P('leaf', 'col'), as said below
- upper_inverse: bfloat16 [16, 1792, 1792], P('leaf', 'col'), as said below
- leaf_update: bfloat16 [16, 4, 1792, 512], P('leaf', None, 'col'), may hold values from -0.0625 to 0.0625
- upper_update: bfloat16 [16, 4, 1792, 512], P('leaf', None, 'col'), may hold values from -0.0625 to 0.0625
- live_rows: int32 [16, 2], P('leaf'), may hold values from 896 to 1792, as said below
- tile_map: int32 [16, 2, 4, 512], P('leaf'), may hold values from 0 to 1791, as said below
Outputs:
- solution: bfloat16 [16, 2, 1792, 128], P('leaf', None, 'col')
Inputs may be any that keep to these rules, and one draw needn't show every extreme that they name: `leaf_inverse`: zero above the diagonal, nonzero on it. `upper_inverse`: zero above the diagonal, nonzero on it. `live_rows`: one supernode has all 1792 rows live and one has 896. `tile_map`: the rows of one tile are distinct and increasing.
All inputs are finite; a program needn't handle non-finite values.
Results may differ from a plain program's by a relative error of at most 0.0075.
Values may be sent and summed in bfloat16 or wider, within the bound.
No kernel may reach another device: no remote copies, remote signals or barrier semaphores. Data moves between devices by JAX's collectives and lax.ppermute only.
A program may use at most 64 MiB of HBM per device.

v0:
```python
import jax
import jax.numpy as jnp
from jax import lax
from jax.sharding import PartitionSpec as P


def forward_solve(inverse_rows, residual, row_mask, active):
    shares = (residual * row_mask).astype(jnp.bfloat16)
    empty = jnp.zeros((inverse_rows.shape[0], residual.shape[1]), jnp.float32)
    shard_rows = lax.all_gather(shares, "col", axis=0, tiled=True)
    solved = lax.cond(
        active,
        lambda: jnp.dot(inverse_rows, shard_rows, preferred_element_type=jnp.float32),
        lambda: empty,
    )
    return (solved * row_mask).astype(jnp.bfloat16)


def tile_terms(update_cols, solved, active):

    def tile_compute():
        return jnp.einsum("srt,rn->stn", update_cols, solved, preferred_element_type=jnp.float32)

    def tile_nothing():
        return jnp.zeros((update_cols.shape[0], update_cols.shape[2], solved.shape[1]), jnp.float32)

    local_terms = lax.cond(active, tile_compute, tile_nothing)
    return lax.psum(local_terms, "col")


def spread(summed, tile_rows, first_row, rows_dev):
    local_rows = tile_rows - first_row
    inside = (local_rows >= 0) & (local_rows < rows_dev)
    target = jnp.where(inside, local_rows, rows_dev)

    def one_slot(values, where_to):
        return (
            jnp.zeros((rows_dev, values.shape[1]), jnp.float32)
            .at[where_to]
            .add(values, mode="drop")
        )

    return jax.vmap(one_slot)(summed, target)


def pick_rows(fetched, tile_rows, first_row, rows_dev):
    local_rows = tile_rows - first_row
    inside = (local_rows >= 0) & (local_rows < rows_dev)
    chosen = fetched[jnp.clip(local_rows, 0, rows_dev - 1)]
    return jnp.where(inside[:, None], chosen, jnp.zeros_like(chosen))


def backward_solve(inverse_rows, solved, pulled, row_mask, active):
    scaled = ((solved.astype(jnp.float32) - pulled) * row_mask).astype(jnp.bfloat16)
    rhs_width = scaled.shape[1]
    row_count = inverse_rows.shape[0] * lax.axis_size("col")

    def rows_compute():
        return lax.dot_general(
            inverse_rows, scaled, (((0,), (0,)), ((), ())), preferred_element_type=jnp.float32
        )

    summed = lax.psum_scatter(
        lax.cond(active, rows_compute, lambda: jnp.zeros((row_count, rhs_width), jnp.float32)),
        "col",
        scatter_dimension=0,
        tiled=True,
    )
    return (summed * row_mask).astype(jnp.bfloat16)


def pull_terms(update_cols, tiles, active):

    def pull_compute():
        return jnp.einsum("srt,stn->rn", update_cols, tiles, preferred_element_type=jnp.float32)

    def pull_nothing():
        return jnp.zeros((update_cols.shape[1], tiles.shape[2]), jnp.float32)

    return lax.cond(active, pull_compute, pull_nothing)


def deliver(outgoing, height, leaf_id, leaf_count):
    owner = leaf_id // 2**height * 2**height + 2 ** (height - 1)
    onehot = (jnp.arange(leaf_count, dtype=jnp.int32) == owner).astype(jnp.float32)
    slot_table = onehot[:, None, None] * outgoing[None]
    return lax.psum_scatter(slot_table, "leaf", scatter_dimension=0, tiled=True)[0]


def fetch(answer_up, height, leaf_id):
    owner = leaf_id // 2**height * 2**height + 2 ** (height - 1)
    gathered = lax.all_gather(answer_up[None], "leaf", axis=0, tiled=True)
    return lax.dynamic_index_in_dim(gathered, owner, 0, keepdims=False)


def shards(
    right_sides, leaf_inverse, upper_inverse, leaf_update, upper_update, live_rows, tile_map
):
    leaf_count = lax.axis_size("leaf")
    depth = leaf_count.bit_length() - 1
    rows_dev = leaf_inverse.shape[1]
    rhs_width = right_sides.shape[3]
    tile_len = tile_map.shape[3]
    leaf_id = lax.axis_index("leaf")
    col_id = lax.axis_index("col")
    first_row = col_id * rows_dev
    row_ids = first_row + jnp.arange(rows_dev, dtype=jnp.int32)
    leaf_mask = (row_ids < live_rows[0, 0]).astype(jnp.float32)[:, None]
    upper_mask = (row_ids < live_rows[0, 1]).astype(jnp.float32)[:, None]
    node_level = jnp.zeros((), jnp.int32)
    for height in range(1, depth + 1):
        node_level = node_level + ((leaf_id % 2 ** (height - 1) == 0) & (leaf_id > 0)).astype(
            jnp.int32
        )
    always = jnp.array(True)
    solved_leaf = forward_solve(
        leaf_inverse[0], right_sides[0, 0].astype(jnp.float32), leaf_mask, always
    )
    summed = tile_terms(leaf_update[0, :depth], solved_leaf, always)
    pieces = spread(summed, tile_map[0, 0, :depth], first_row, rows_dev)
    outgoing = [None] + [pieces[height - 1] for height in range(1, depth + 1)]
    residual_up = right_sides[0, 1].astype(jnp.float32)
    solved_up = jnp.zeros((rows_dev, rhs_width), jnp.bfloat16)
    for height in range(1, depth + 1):
        residual_up = residual_up - deliver(outgoing[height], height, leaf_id, leaf_count)
        active = node_level == height
        solved = forward_solve(upper_inverse[0], residual_up, upper_mask, active)
        solved_up = jnp.where(active, solved, solved_up)
        slot_count = depth - height
        if slot_count > 0:
            summed = tile_terms(upper_update[0, :slot_count], solved, active)
            pieces = spread(summed, tile_map[0, 1, :slot_count], first_row, rows_dev)
            for slot_idx in range(slot_count):
                outgoing[height + 1 + slot_idx] = outgoing[height + 1 + slot_idx] + pieces[slot_idx]
    answer_up = jnp.zeros((rows_dev, rhs_width), jnp.bfloat16)
    tiles_leaf = [None] * depth
    tiles_upper = jnp.zeros((depth, tile_len, rhs_width), jnp.bfloat16)
    for height in range(depth, 0, -1):
        active = node_level == height
        slot_count = depth - height
        if slot_count > 0:
            pulled = pull_terms(upper_update[0, :slot_count], tiles_upper[:slot_count], active)
        else:
            pulled = jnp.zeros((rows_dev, rhs_width), jnp.float32)
        answer = backward_solve(upper_inverse[0], solved_up, pulled, upper_mask, active)
        answer_up = jnp.where(active, answer, answer_up)
        fetched = fetch(answer_up, height, leaf_id)
        slot_now = jnp.clip(height - node_level - 1, 0, depth - 1)
        valid = (node_level > 0) & (node_level < height)
        upper_map = lax.dynamic_index_in_dim(tile_map[0, 1], slot_now, 0, keepdims=False)
        leaf_part = pick_rows(fetched, tile_map[0, 0, height - 1], first_row, rows_dev)
        upper_part = pick_rows(fetched, upper_map, first_row, rows_dev)
        upper_part = jnp.where(valid, upper_part, jnp.zeros_like(upper_part))
        both = (
            lax.psum(jnp.stack([leaf_part, upper_part]), "col")
            .astype(jnp.float32)
            .astype(jnp.bfloat16)
        )
        tiles_leaf[height - 1] = both[0]
        updated = lax.dynamic_update_index_in_dim(tiles_upper, both[1], slot_now, 0)
        tiles_upper = jnp.where(valid, updated, tiles_upper)
    pulled = pull_terms(leaf_update[0, :depth], jnp.stack(tiles_leaf), always)
    answer_leaf = backward_solve(leaf_inverse[0], solved_leaf, pulled, leaf_mask, always)
    return jnp.stack([answer_leaf, answer_up])[None]


def solution(mesh):
    placed = (
        P("leaf", None, "col", None),
        P("leaf", "col", None),
        P("leaf", "col", None),
        P("leaf", None, "col", None),
        P("leaf", None, "col", None),
        P("leaf", None),
        P("leaf", None, None, None),
    )
    return jax.shard_map(
        shards, mesh=mesh, in_specs=placed, out_specs=P("leaf", None, "col", None), check_vma=False
    )
```

profile of v0, /device:TPU:4, one launch (start us, length us, event | category | flops | bytes accessed | tf_op | source)
XLA Modules:
  0.0 1755.9 jit_solution(690837087671866343)
XLA Ops:
  6.5 1.4 fusion.78
  9.4 21.2 %all_gather.27 = bf16[1792,128]{1,0:T(8,128)(2,1)S(1)} all-gather(bf16[112,128]{1,0:T(8,128)(2,1)S(1)} %fusion.53), channel_id=1, replica_groups=mesh['leaf'=16,'col'=16] {'col'}, dimensions={0}, use_global_device_ids=true | all-gather | bytes 487424 | tf_op jit(solution)/shard_map/all_gather | solution.py:10
  31.0 1.3 convolution_bitcast_fusion.4
  34.5 108.2 %all-reduce.13.cloned.1.call-done = f32[4,512,128]{1,2,0:T(8,128)} async-done(((f32[4,512,128]{1,2,0:T(8,128)}), f32[4,512,128]{1,2,0:T(8,128)}) %all-reduce.13.cloned.1.call-update) | async-done | bytes 1048592 | tf_op jit(solution)/shard_map/psum | solution.py:28
  142.7 1.5 copy.73
  144.3 11.5 scatter_custom_fusion.1
  155.8 1.1 broadcast_multiply_fusion.3
  158.6 77.5 %reduce-scatter.38.cloned.1.call-done = f32[1,112,128]{2,1,0:T(8,128)} async-done(((f32[16,112,128]{2,1,0:T(8,128)}), f32[1,112,128]{2,1,0:T(8,128)}) %reduce-scatter.38.cloned.1.call-update) | async-done | bytes 57360
  237.0 18.7 %all_gather.28 = bf16[1792,128]{1,0:T(8,128)(2,1)S(1)} all-gather(bf16[112,128]{1,0:T(8,128)(2,1)S(1)} %multiply_convert_fusion.11), channel_id=1, replica_groups=mesh['leaf'=16,'col'=16] {'col'}, dimensions={0}, use_global_device_ids=true | all-gather | bytes 487424 | tf_op jit(solution)/shard_map/all_gather | solution.py:10
  257.0 109.0 %all-reduce.15.cloned.1.call-done = f32[3,512,128]{2,1,0:T(8,128)} async-done(((f32[3,512,128]{2,1,0:T(8,128)}), f32[3,512,128]{2,1,0:T(8,128)}) %all-reduce.15.cloned.1.call-update) | async-done | bytes 786448 | tf_op jit(solution)/shard_map/psum | solution.py:28
  366.0 9.1 scatter_custom_fusion.2
  375.1 1.1 broadcast_multiply_fusion.2
  377.1 78.3 %reduce-scatter.40.cloned.1.call-done = f32[1,112,128]{2,1,0:T(8,128)} async-done(((f32[16,112,128]{2,1,0:T(8,128)}), f32[1,112,128]{2,1,0:T(8,128)}) %reduce-scatter.40.cloned.1.call-update) | async-done | bytes 57360
  456.3 18.7 %all_gather.29 = bf16[1792,128]{1,0:T(8,128)(2,1)S(1)} all-gather(bf16[112,128]{1,0:T(8,128)(2,1)S(1)} %get-tuple-element.234), channel_id=1, replica_groups=mesh['leaf'=16,'col'=16] {'col'}, dimensions={0}, use_global_device_ids=true | all-gather | bytes 487424 | tf_op jit(solution)/shard_map/all_gather | solution.py:10
  476.6 107.9 %all-reduce.17.cloned.1.call-done = f32[2,512,128]{2,1,0:T(8,128)} async-done(((f32[2,512,128]{2,1,0:T(8,128)}), f32[2,512,128]{2,1,0:T(8,128)}) %all-reduce.17.cloned.1.call-update) | async-done | bytes 524304 | tf_op jit(solution)/shard_map/psum | solution.py:28
  584.4 6.4 scatter_custom_fusion.3
  590.9 1.1 broadcast_multiply_fusion.1
  592.1 79.1 %reduce-scatter.42.cloned.1.call-done = f32[1,112,128]{2,1,0:T(8,128)} async-done(((f32[16,112,128]{2,1,0:T(8,128)}), f32[1,112,128]{2,1,0:T(8,128)}) %reduce-scatter.42.cloned.1.call-update) | async-done | bytes 57360
  672.2 18.7 %all_gather.30 = bf16[1792,128]{1,0:T(8,128)(2,1)S(1)} all-gather(bf16[112,128]{1,0:T(8,128)(2,1)S(1)} %multiply_convert_fusion.7), channel_id=1, replica_groups=mesh['leaf'=16,'col'=16] {'col'}, dimensions={0}, use_global_device_ids=true | all-gather | bytes 487424 | tf_op jit(solution)/shard_map/all_gather | solution.py:10
  691.8 106.9 %all-reduce.19.cloned.1.call-done = f32[1,512,128]{2,1,0:T(8,128)} async-done(((f32[1,512,128]{2,1,0:T(8,128)}), f32[1,512,128]{2,1,0:T(8,128)}) %all-reduce.19.cloned.1.call-update) | async-done | bytes 262160 | tf_op jit(solution)/shard_map/psum | solution.py:28
  798.7 3.9 scatter_custom_fusion
  802.6 1.1 broadcast_multiply_fusion
  803.8 79.3 %reduce-scatter.44.cloned.1.call-done = f32[1,112,128]{2,1,0:T(8,128)} async-done(((f32[16,112,128]{2,1,0:T(8,128)}), f32[1,112,128]{2,1,0:T(8,128)}) %reduce-scatter.44.cloned.1.call-update) | async-done | bytes 57360
  884.0 18.7 %all_gather.31 = bf16[1792,128]{1,0:T(8,128)(2,1)S(1)} all-gather(bf16[112,128]{1,0:T(8,128)(2,1)S(1)} %fusion.55), channel_id=1, replica_groups=mesh['leaf'=16,'col'=16] {'col'}, dimensions={0}, use_global_device_ids=true | all-gather | bytes 487424 | tf_op jit(solution)/shard_map/all_gather | solution.py:10
  902.9 0.9 copy-done.2
  906.3 52.8 %reduce-scatter.28.cloned.1.call-done = f32[112,128]{1,0:T(8,128)} async-done(((f32[1792,128]{1,0:T(8,128)}), f32[112,128]{1,0:T(8,128)}) %reduce-scatter.28.cloned.1.call-update) | async-done | bytes 57360 | tf_op jit(solution)/shard_map/reduce_scatter | solution.py:63
  960.0 23.5 %all-gather = bf16[1792,128]{1,0:T(8,128)(2,1)S(1)} all-gather(bf16[112,128]{1,0:T(8,128)(2,1)S(1)} %fusion.60), channel_id=2, replica_groups=mesh['leaf'=16,'col'=16] {'leaf'}, dimensions={0}, use_global_device_ids=true | all-gather | bytes 487424 | tf_op jit(solution)/shard_map/all_gather | solution.py:92
  983.6 1.3 gather_fusion.1
  984.9 1.3 gather_fusion
  987.3 107.1 %all-reduce.21.cloned.1.call-done = bf16[2,512,128]{2,1,0:T(8,128)(2,1)} async-done(((bf16[2,512,128]{2,1,0:T(8,128)(2,1)}), bf16[2,512,128]{2,1,0:T(8,128)(2,1)}) %all-reduce.21.cloned.1.call-update) | async-done | bytes 262160 | tf_op jit(solution)/shard_map/psum | solution.py:155
  1096.6 58.6 %reduce-scatter.30.cloned.1.call-done = f32[112,128]{1,0:T(8,128)} async-done(((f32[1792,128]{1,0:T(8,128)}), f32[112,128]{1,0:T(8,128)}) %reduce-scatter.30.cloned.1.call-update) | async-done | bytes 57360 | tf_op jit(solution)/shard_map/reduce_scatter | solution.py:63
  1156.2 23.6 %all-gather.1 = bf16[1792,128]{1,0:T(8,128)(2,1)S(1)} all-gather(bf16[112,128]{1,0:T(8,128)(2,1)S(1)} %fusion.61), channel_id=3, replica_groups=mesh['leaf'=16,'col'=16] {'leaf'}, dimensions={0}, use_global_device_ids=true | all-gather | bytes 487424 | tf_op jit(solution)/shard_map/all_gather | solution.py:92
  1179.8 1.3 gather_fusion.2
  1181.1 1.3 gather_fusion.3
  1183.5 107.0 %all-reduce.23.cloned.1.call-done = bf16[2,512,128]{2,1,0:T(8,128)(2,1)} async-done(((bf16[2,512,128]{2,1,0:T(8,128)(2,1)}), bf16[2,512,128]{2,1,0:T(8,128)(2,1)}) %all-reduce.23.cloned.1.call-update) | async-done | bytes 262160 | tf_op jit(solution)/shard_map/psum | solution.py:155
  1290.6 1.0 fusion.76
  1293.9 58.4 %reduce-scatter.32.cloned.1.call-done = f32[112,128]{1,0:T(8,128)} async-done(((f32[1792,128]{1,0:T(8,128)}), f32[112,128]{1,0:T(8,128)}) %reduce-scatter.32.cloned.1.call-update) | async-done | bytes 57360 | tf_op jit(solution)/shard_map/reduce_scatter | solution.py:63
  1353.1 23.6 %all-gather.2 = bf16[1792,128]{1,0:T(8,128)(2,1)S(1)} all-gather(bf16[112,128]{1,0:T(8,128)(2,1)S(1)} %fusion.62), channel_id=4, replica_groups=mesh['leaf'=16,'col'=16] {'leaf'}, dimensions={0}, use_global_device_ids=true | all-gather | bytes 487424 | tf_op jit(solution)/shard_map/all_gather | solution.py:92
  1376.7 1.3 gather_fusion.4
  1378.1 1.3 gather_fusion.5
  1381.7 107.2 %all-reduce.25.cloned.1.call-done = bf16[2,512,128]{2,1,0:T(8,128)(2,1)} async-done(((bf16[2,512,128]{2,1,0:T(8,128)(2,1)}), bf16[2,512,128]{2,1,0:T(8,128)(2,1)}) %all-reduce.25.cloned.1.call-update) | async-done | bytes 262160 | tf_op jit(solution)/shard_map/psum | solution.py:155
  1491.0 58.9 %reduce-scatter.34.cloned.1.call-done = f32[112,128]{1,0:T(8,128)} async-done(((f32[1792,128]{1,0:T(8,128)}), f32[112,128]{1,0:T(8,128)}) %reduce-scatter.34.cloned.1.call-update) | async-done | bytes 57360 | tf_op jit(solution)/shard_map/reduce_scatter | solution.py:63
  1550.7 23.6 %all-gather.3 = bf16[1792,128]{1,0:T(8,128)(2,1)S(1)} all-gather(bf16[112,128]{1,0:T(8,128)(2,1)S(1)} %fusion.63), channel_id=5, replica_groups=mesh['leaf'=16,'col'=16] {'leaf'}, dimensions={0}, use_global_device_ids=true | all-gather | bytes 487424 | tf_op jit(solution)/shard_map/all_gather | solution.py:92
  1574.3 1.3 gather_fusion.6
  1575.7 1.3 gather_fusion.7
  1580.2 106.1 %all-reduce.27.cloned.1.call-done = bf16[2,512,128]{2,1,0:T(8,128)(2,1)} async-done(((bf16[2,512,128]{2,1,0:T(8,128)(2,1)}), bf16[2,512,128]{2,1,0:T(8,128)(2,1)}) %all-reduce.27.cloned.1.call-update) | async-done | bytes 262160 | tf_op jit(solution)/shard_map/psum | solution.py:155
  1687.8 1.2 copy.91
  1689.1 58.7 %reduce-scatter.36.cloned.1.call-done = f32[112,128]{1,0:T(8,128)} async-done(((f32[1792,128]{1,0:T(8,128)}), f32[112,128]{1,0:T(8,128)}) %reduce-scatter.36.cloned.1.call-update) | async-done | bytes 57360 | tf_op jit(solution)/shard_map/reduce_scatter | solution.py:63
  (217 shorter events, 38.0 us)
Async XLA Ops:
  6.5 24.4 %copy-start = (bf16[1,4,112,512]{3,2,1,0:T(8,128)(2,1)S(1)}, bf16[1,4,112,512]{3,2,1,0:T(8,128)(2,1)}, u32[]{:S(2)}) copy-start(bf16[1,4,112,512]{3,2,1,0:T(8,128)(2,1)} %param.38) | copy-start | bytes 1376260
  6.5 24.1 %copy-start.8 = (bf16[1,112,1792]{2,1,0:T(8,128)(2,1)S(1)}, bf16[1,112,1792]{2,1,0:T(8,128)(2,1)}, u32[]{:S(2)}) copy-start(bf16[1,112,1792]{2,1,0:T(8,128)(2,1)} %param.36) | copy-start | bytes 1204228
  6.5 136.2 %all-reduce.13.cloned.1.call-start = ((), (), s32[]{:S(2)}) async-start(), calls=%async_computation.9 | async-start | bytes 2097152 | tf_op jit(solution)/shard_map/psum | solution.py:28
  31.0 1.3 copy-start.16
  32.3 203.8 %reduce-scatter.38.cloned.1.call-start = ((), (), s32[]{:S(2)}) async-start(), calls=%async_computation.22 | async-start | bytes 974848
  32.3 0.7 copy-start.23
  33.1 0.7 copy-start.27
  156.9 1.6 copy-start.10
  156.9 209.0 %all-reduce.15.cloned.1.call-start = ((), (), s32[]{:S(2)}) async-start(), calls=%async_computation.10 | async-start | bytes 1572864 | tf_op jit(solution)/shard_map/psum | solution.py:28
  158.5 77.6 %copy-start.24 = (bf16[1,2,112,128]{3,2,1,0:T(8,128)(2,1)S(1)}, bf16[1,2,112,128]{3,2,1,0:T(8,128)(2,1)}, u32[]{:S(2)}) copy-start(bf16[1,2,112,128]{3,2,1,0:T(8,128)(2,1)} %param.35) | copy-start | bytes 172036
  158.6 97.1 %copy-start.1 = (bf16[1,112,1792]{2,1,0:T(8,128)(2,1)S(1)}, bf16[1,112,1792]{2,1,0:T(8,128)(2,1)}, u32[]{:S(2)}) copy-start(bf16[1,112,1792]{2,1,0:T(8,128)(2,1)} %param.37) | copy-start | bytes 1204228
  255.9 0.9 copy-start.6
  256.8 198.6 %reduce-scatter.40.cloned.1.call-start = ((), (), s32[]{:S(2)}) async-start(), calls=%async_computation.23 | async-start | bytes 974848
  376.2 208.2 %all-reduce.17.cloned.1.call-start = ((), (), s32[]{:S(2)}) async-start(), calls=%async_computation.11 | async-start | bytes 1048576 | tf_op jit(solution)/shard_map/psum | solution.py:28
  376.3 0.7 copy-start.34
  377.1 78.4 %copy-start.20 = (f32[1,112,128]{2,1,0:T(8,128)S(1)}, f32[1,112,128]{2,1,0:T(8,128)}, u32[]{:S(2)}) copy-start(f32[1,112,128]{2,1,0:T(8,128)} %reduce-scatter.38.cloned.1.call-done) | copy-start | bytes 172036
  475.7 0.8 copy-start.7
  476.5 194.8 %reduce-scatter.42.cloned.1.call-start = ((), (), s32[]{:S(2)}) async-start(), calls=%async_computation.24 | async-start | bytes 974848
  592.0 206.7 %all-reduce.19.cloned.1.call-start = ((), (), s32[]{:S(2)}) async-start(), calls=%async_computation.12 | async-start | bytes 524288 | tf_op jit(solution)/shard_map/psum | solution.py:28
  691.0 0.7 copy-start.9
  691.7 191.4 %reduce-scatter.44.cloned.1.call-start = ((), (), s32[]{:S(2)}) async-start(), calls=%async_computation.25 | async-start | bytes 974848
  803.7 79.4 %copy-start.22 = (f32[1,112,128]{2,1,0:T(8,128)S(1)}, f32[1,112,128]{2,1,0:T(8,128)}, u32[]{:S(2)}) copy-start(f32[1,112,128]{2,1,0:T(8,128)} %reduce-scatter.42.cloned.1.call-done) | copy-start | bytes 172036
  803.7 155.4 %reduce-scatter.28.cloned.1.call-start = ((), (), s32[]{:S(2)}) async-start(), calls=%async_computation.17 | async-start | bytes 974848 | tf_op jit(solution)/shard_map/reduce_scatter | solution.py:63
  902.8 192.6 %copy-start.11 = (bf16[112,128]{1,0:T(8,128)(2,1)}, bf16[112,128]{1,0:T(8,128)(2,1)S(1)}, u32[]{:S(2)}) copy-start(bf16[112,128]{1,0:T(8,128)(2,1)S(1)} %get-tuple-element.233) | copy-start | bytes 86020
  902.9 0.9 copy-start.2
  903.8 190.5 %all-reduce.21.cloned.1.call-start = ((), (), s32[]{:S(2)}) async-start(), calls=%async_computation.13 | async-start | bytes 524288 | tf_op jit(solution)/shard_map/psum | solution.py:155
  987.2 168.0 %reduce-scatter.30.cloned.1.call-start = ((), (), s32[]{:S(2)}) async-start(), calls=%async_computation.18 | async-start | bytes 974848 | tf_op jit(solution)/shard_map/reduce_scatter | solution.py:63
  1094.3 0.9 copy-start.15
  1095.6 0.9 copy-start.3
  1095.6 59.7 %copy-start.21 = (f32[112,128]{1,0:T(8,128)S(1)}, f32[112,128]{1,0:T(8,128)}, u32[]{:S(2)}) copy-start(f32[112,128]{1,0:T(8,128)} %reduce-scatter.28.cloned.1.call-done) | copy-start | bytes 172036
  1096.5 194.1 %all-reduce.23.cloned.1.call-start = ((), (), s32[]{:S(2)}) async-start(), calls=%async_computation.14 | async-start | bytes 524288 | tf_op jit(solution)/shard_map/psum | solution.py:155
  1156.1 23.6 %copy-start.18 = (bf16[112,128]{1,0:T(8,128)(2,1)}, bf16[112,128]{1,0:T(8,128)(2,1)S(1)}, u32[]{:S(2)}) copy-start(bf16[112,128]{1,0:T(8,128)(2,1)S(1)} %fusion.61) | copy-start | bytes 86020
  1183.5 168.7 %reduce-scatter.32.cloned.1.call-start = ((), (), s32[]{:S(2)}) async-start(), calls=%async_computation.19 | async-start | bytes 974848 | tf_op jit(solution)/shard_map/reduce_scatter | solution.py:63
  1291.6 0.7 copy-start.12
  1292.8 0.9 copy-start.4
  1292.8 1.0 copy-start.26
  1292.8 1.1 copy-start.25
  1293.7 58.5 %copy-start.19 = (bf16[112,128]{1,0:T(8,128)(2,1)S(1)}, bf16[112,128]{1,0:T(8,128)(2,1)}, u32[]{:S(2)}) copy-start(bf16[112,128]{1,0:T(8,128)(2,1)} %copy-done.18) | copy-start | bytes 86020
  1293.8 195.2 %all-reduce.25.cloned.1.call-start = ((), (), s32[]{:S(2)}) async-start(), calls=%async_computation.15 | async-start | bytes 524288 | tf_op jit(solution)/shard_map/psum | solution.py:155
  1381.7 168.1 %reduce-scatter.34.cloned.1.call-start = ((), (), s32[]{:S(2)}) async-start(), calls=%async_computation.20 | async-start | bytes 974848 | tf_op jit(solution)/shard_map/reduce_scatter | solution.py:63
  1489.0 0.7 copy-start.13
  1489.9 0.9 copy-start.5
  1490.9 195.5 %all-reduce.27.cloned.1.call-start = ((), (), s32[]{:S(2)}) async-start(), calls=%async_computation.16 | async-start | bytes 524288 | tf_op jit(solution)/shard_map/psum | solution.py:155
  1577.7 0.7 copy-start.28
  1579.3 0.9 copy-start.14
  1579.3 168.5 %reduce-scatter.36.cloned.1.call-start = ((), (), s32[]{:S(2)}) async-start(), calls=%async_computation.21 | async-start | bytes 974848 | tf_op jit(solution)/shard_map/reduce_scatter | solution.py:63
  1580.2 106.1 %copy-start.17 = (bf16[128,112]{0,1:T(8,128)(2,1)S(1)}, bf16[128,112]{0,1:T(8,128)(2,1)}, u32[]{:S(2)}) copy-start(bf16[128,112]{0,1:T(8,128)(2,1)} %copy-done.16) | copy-start | bytes 86020
  1686.4 0.9 slice-start
  (5 other events, 3.1 us)
Sparse Core Ops, SparseCore 0:
  32.4 110.2 all-reduce.12
  157.1 78.9 reduce-scatter.37
  256.9 108.9 all-reduce.14
  376.3 79.0 reduce-scatter.39
  476.6 107.7 all-reduce.16
  592.1 79.0 reduce-scatter.41
  691.8 106.8 all-reduce.18
  803.8 79.1 reduce-scatter.43
  903.9 55.1 reduce-scatter.27
  987.3 106.9 all-reduce.20
  1096.9 58.3 reduce-scatter.29
  1183.6 106.9 all-reduce.22
  1293.9 58.3 reduce-scatter.31
  1381.8 107.1 all-reduce.24
  1491.3 58.4 reduce-scatter.33
  1579.4 106.9 all-reduce.26
  1689.2 58.5 reduce-scatter.35
where the time goes:
time: 1760 us
  waiting for transfers between devices  1460 us (83%)
  blocking collectives  190 us (11%)
  other arithmetic  54.8 us (3%)
  local copies, waits for them, and re-layouts  31.1 us (2%)
    psum x4, waiting for transfers between devices, tile_terms(): return lax.psum(local_terms, 'col')  432 us
    psum x4, waiting for transfers between devices, shards(): lax.psum(jnp.stack([leaf_part, upper_part]), 'col').astype(jnp.float32)  427 us
    unnamed x21, waiting for transfers between devices  315 us
    reduce_scatter x5, waiting for transfers between devices, backward_solve(): lax.psum_scatter(lax.cond(active, rows_compute, lambda: jnp.zeros((row_co...  287 us
    all_gather x5, blocking collectives, forward_solve(): shard_rows = lax.all_gather(shares, 'col', axis=0, tiled=True)  96 us
    all_gather x4, blocking collectives, fetch(): gathered = lax.all_gather(answer_up[None], 'leaf', axis=0, tiled=True)  94.3 us
  transfers between devices with their start and end apart: 17, of which 17 were waited for; matrix products, arithmetic and copies ran while one was open for 0% of the time, Pallas kernels for 0%

commit v1 on v0

--- a/solution.py
+++ b/solution.py
@@ -25,7 +25,7 @@
         return jnp.zeros((update_cols.shape[0], update_cols.shape[2], solved.shape[1]), jnp.float32)
 
     local_terms = lax.cond(active, tile_compute, tile_nothing)
-    return lax.psum(local_terms, "col")
+    return jnp.sum(lax.all_gather(local_terms, "col"), axis=0)
 
 
 def spread(summed, tile_rows, first_row, rows_dev):

time: 1760 us -> 1590 us (0.903)
  waiting for transfers between devices: 1460 us -> 1280 us
  other arithmetic: 54.8 us -> 81.3 us
    psum x4 -> x0, waiting for transfers between devices: 432 us -> none  [tile_terms(): return lax.psum(local_terms, 'col')]
    all_gather x0 -> x4, waiting for transfers between devices: none -> 256 us  [tile_terms(): return jnp.sum(lax.all_gather(local_terms, 'col'), axis=0)]
    reduce_sum x0 -> x4, other arithmetic: none -> 18.2 us  [tile_terms(): return jnp.sum(lax.all_gather(local_terms, 'col'), axis=0)]
where the time goes in v1:
time: 1590 us
  waiting for transfers between devices  1280 us (81%)
  blocking collectives  190 us (12%)
  other arithmetic  81.3 us (5%)
  local copies, waits for them, and re-layouts  23.9 us (2%)
    psum x4, waiting for transfers between devices, shards(): lax.psum(jnp.stack([leaf_part, upper_part]), 'col').astype(jnp.float32)  427 us
    unnamed x21, waiting for transfers between devices  309 us
    reduce_scatter x5, waiting for transfers between devices, backward_solve(): lax.psum_scatter(lax.cond(active, rows_compute, lambda: jnp.zeros((row_co...  287 us
    all_gather x4, waiting for transfers between devices, tile_terms(): return jnp.sum(lax.all_gather(local_terms, 'col'), axis=0)  256 us
    all_gather x5, blocking collectives, forward_solve(): shard_rows = lax.all_gather(shares, 'col', axis=0, tiled=True)  95.9 us
    all_gather x4, blocking collectives, fetch(): gathered = lax.all_gather(answer_up[None], 'leaf', axis=0, tiled=True)  94 us
  transfers between devices with their start and end apart: 17, of which 17 were waited for; matrix products, arithmetic and copies ran while one was open for 0% of the time, Pallas kernels for 0%

profile of v1, /device:TPU:4, one launch (start us, length us, event | category | flops | bytes accessed | tf_op | source)
XLA Modules:
  0.0 1592.5 jit_solution(1535010778906564018)
XLA Ops:
  6.5 1.4 fusion.76
  9.4 21.2 %all_gather.51 = bf16[1792,128]{1,0:T(8,128)(2,1)S(1)} all-gather(bf16[112,128]{1,0:T(8,128)(2,1)S(1)} %fusion.51), channel_id=1, replica_groups=mesh['leaf'=16,'col'=16] {'col'}, dimensions={0}, use_global_device_ids=true | all-gather | bytes 487424 | tf_op jit(solution)/shard_map/all_gather | solution.py:10
  30.6 1.3 fusion.14
  32.8 1.3 copy.81
  36.5 91.3 %all-gather.13.cloned.1.call-done = f32[64,512,128]{2,1,0:T(8,128)} async-done(((f32[4,512,128]{2,1,0:T(8,128)}), f32[64,512,128]{2,1,0:T(8,128)}) %all-gather.13.cloned.1.call-update) | async-done | bytes 16777232 | tf_op jit(solution)/shard_map/all_gather | solution.py:28
  127.8 6.7 reduce_sum.38
  134.5 11.5 scatter_custom_fusion.1
  146.0 1.1 broadcast_multiply_fusion.3
  147.9 76.6 %reduce-scatter.38.cloned.1.call-done = f32[1,112,128]{2,1,0:T(8,128)} async-done(((f32[16,112,128]{2,1,0:T(8,128)}), f32[1,112,128]{2,1,0:T(8,128)}) %reduce-scatter.38.cloned.1.call-update) | async-done | bytes 57360
  225.5 18.7 %all_gather.54 = bf16[1792,128]{1,0:T(8,128)(2,1)S(1)} all-gather(bf16[112,128]{1,0:T(8,128)(2,1)S(1)} %multiply_convert_fusion.11), channel_id=1, replica_groups=mesh['leaf'=16,'col'=16] {'col'}, dimensions={0}, use_global_device_ids=true | all-gather | bytes 487424 | tf_op jit(solution)/shard_map/all_gather | solution.py:10
  245.7 72.7 %all-gather.15.cloned.1.call-done = f32[48,512,128]{2,1,0:T(8,128)} async-done(((f32[3,512,128]{2,1,0:T(8,128)}), f32[48,512,128]{2,1,0:T(8,128)}) %all-gather.15.cloned.1.call-update) | async-done | bytes 12582928 | tf_op jit(solution)/shard_map/all_gather | solution.py:28
  318.4 5.3 reduce_sum.39
  323.7 8.8 scatter_custom_fusion.2
  333.7 77.3 %reduce-scatter.40.cloned.1.call-done = f32[1,112,128]{2,1,0:T(8,128)} async-done(((f32[16,112,128]{2,1,0:T(8,128)}), f32[1,112,128]{2,1,0:T(8,128)}) %reduce-scatter.40.cloned.1.call-update) | async-done | bytes 57360
  411.9 18.7 %all_gather.57 = bf16[1792,128]{1,0:T(8,128)(2,1)S(1)} all-gather(bf16[112,128]{1,0:T(8,128)(2,1)S(1)} %get-tuple-element.234), channel_id=1, replica_groups=mesh['leaf'=16,'col'=16] {'col'}, dimensions={0}, use_global_device_ids=true | all-gather | bytes 487424 | tf_op jit(solution)/shard_map/all_gather | solution.py:10
  432.4 52.8 %all-gather.17.cloned.1.call-done = f32[32,512,128]{2,1,0:T(8,128)} async-done(((f32[2,512,128]{2,1,0:T(8,128)}), f32[32,512,128]{2,1,0:T(8,128)}) %all-gather.17.cloned.1.call-update) | async-done | bytes 8388624 | tf_op jit(solution)/shard_map/all_gather | solution.py:28
  485.2 3.8 reduce_sum.40
  489.0 6.0 scatter_custom_fusion.3
  496.2 77.4 %reduce-scatter.42.cloned.1.call-done = f32[1,112,128]{2,1,0:T(8,128)} async-done(((f32[16,112,128]{2,1,0:T(8,128)}), f32[1,112,128]{2,1,0:T(8,128)}) %reduce-scatter.42.cloned.1.call-update) | async-done | bytes 57360
  574.6 18.7 %all_gather.60 = bf16[1792,128]{1,0:T(8,128)(2,1)S(1)} all-gather(bf16[112,128]{1,0:T(8,128)(2,1)S(1)} %multiply_convert_fusion.7), channel_id=1, replica_groups=mesh['leaf'=16,'col'=16] {'col'}, dimensions={0}, use_global_device_ids=true | all-gather | bytes 487424 | tf_op jit(solution)/shard_map/all_gather | solution.py:10
  594.4 38.8 %all-gather.19.cloned.1.call-done = f32[16,512,128]{2,1,0:T(8,128)} async-done(((f32[1,512,128]{2,1,0:T(8,128)}), f32[16,512,128]{2,1,0:T(8,128)}) %all-gather.19.cloned.1.call-update) | async-done | bytes 4194320 | tf_op jit(solution)/shard_map/all_gather | solution.py:28
  633.2 2.4 reduce.7
  635.7 3.3 scatter_fusion
  640.1 77.4 %reduce-scatter.44.cloned.1.call-done = f32[1,112,128]{2,1,0:T(8,128)} async-done(((f32[16,112,128]{2,1,0:T(8,128)}), f32[1,112,128]{2,1,0:T(8,128)}) %reduce-scatter.44.cloned.1.call-update) | async-done | bytes 57360
  718.4 18.7 %all_gather.63 = bf16[1792,128]{1,0:T(8,128)(2,1)S(1)} all-gather(bf16[112,128]{1,0:T(8,128)(2,1)S(1)} %fusion.53), channel_id=1, replica_groups=mesh['leaf'=16,'col'=16] {'col'}, dimensions={0}, use_global_device_ids=true | all-gather | bytes 487424 | tf_op jit(solution)/shard_map/all_gather | solution.py:10
  740.7 52.7 %reduce-scatter.28.cloned.1.call-done = f32[112,128]{1,0:T(8,128)} async-done(((f32[1792,128]{1,0:T(8,128)}), f32[112,128]{1,0:T(8,128)}) %reduce-scatter.28.cloned.1.call-update) | async-done | bytes 57360 | tf_op jit(solution)/shard_map/reduce_scatter | solution.py:63
  794.3 23.5 %all-gather.4 = bf16[1792,128]{1,0:T(8,128)(2,1)S(1)} all-gather(bf16[112,128]{1,0:T(8,128)(2,1)S(1)} %fusion.58), channel_id=6, replica_groups=mesh['leaf'=16,'col'=16] {'leaf'}, dimensions={0}, use_global_device_ids=true | all-gather | bytes 487424 | tf_op jit(solution)/shard_map/all_gather | solution.py:92
  817.9 1.3 gather_fusion.1
  819.2 1.3 gather_fusion
  821.6 107.1 %all-reduce.9.cloned.1.call-done = bf16[2,512,128]{2,1,0:T(8,128)(2,1)} async-done(((bf16[2,512,128]{2,1,0:T(8,128)(2,1)}), bf16[2,512,128]{2,1,0:T(8,128)(2,1)}) %all-reduce.9.cloned.1.call-update) | async-done | bytes 262160 | tf_op jit(solution)/shard_map/psum | solution.py:155
  931.0 58.5 %reduce-scatter.30.cloned.1.call-done = f32[112,128]{1,0:T(8,128)} async-done(((f32[1792,128]{1,0:T(8,128)}), f32[112,128]{1,0:T(8,128)}) %reduce-scatter.30.cloned.1.call-update) | async-done | bytes 57360 | tf_op jit(solution)/shard_map/reduce_scatter | solution.py:63
  990.5 23.6 %all-gather.5 = bf16[1792,128]{1,0:T(8,128)(2,1)S(1)} all-gather(bf16[112,128]{1,0:T(8,128)(2,1)S(1)} %fusion.59), channel_id=7, replica_groups=mesh['leaf'=16,'col'=16] {'leaf'}, dimensions={0}, use_global_device_ids=true | all-gather | bytes 487424 | tf_op jit(solution)/shard_map/all_gather | solution.py:92
  1014.1 1.3 gather_fusion.2
  1015.4 1.3 gather_fusion.3
  1019.1 107.0 %all-reduce.11.cloned.1.call-done = bf16[2,512,128]{2,1,0:T(8,128)(2,1)} async-done(((bf16[2,512,128]{2,1,0:T(8,128)(2,1)}), bf16[2,512,128]{2,1,0:T(8,128)(2,1)}) %all-reduce.11.cloned.1.call-update) | async-done | bytes 262160 | tf_op jit(solution)/shard_map/psum | solution.py:155
  1130.9 57.3 %reduce-scatter.32.cloned.1.call-done = f32[112,128]{1,0:T(8,128)} async-done(((f32[1792,128]{1,0:T(8,128)}), f32[112,128]{1,0:T(8,128)}) %reduce-scatter.32.cloned.1.call-update) | async-done | bytes 57360 | tf_op jit(solution)/shard_map/reduce_scatter | solution.py:63
  1189.1 23.4 %all-gather.6 = bf16[1792,128]{1,0:T(8,128)(2,1)S(1)} all-gather(bf16[112,128]{1,0:T(8,128)(2,1)S(1)} %fusion.60), channel_id=8, replica_groups=mesh['leaf'=16,'col'=16] {'leaf'}, dimensions={0}, use_global_device_ids=true | all-gather | bytes 487424 | tf_op jit(solution)/shard_map/all_gather | solution.py:92
  1212.5 1.3 gather_fusion.4
  1213.8 1.3 gather_fusion.5
  1217.5 107.0 %all-reduce.13.cloned.1.call-done = bf16[2,512,128]{2,1,0:T(8,128)(2,1)} async-done(((bf16[2,512,128]{2,1,0:T(8,128)(2,1)}), bf16[2,512,128]{2,1,0:T(8,128)(2,1)}) %all-reduce.13.cloned.1.call-update) | async-done | bytes 262160 | tf_op jit(solution)/shard_map/psum | solution.py:155
  1326.5 59.6 %reduce-scatter.34.cloned.1.call-done = f32[112,128]{1,0:T(8,128)} async-done(((f32[1792,128]{1,0:T(8,128)}), f32[112,128]{1,0:T(8,128)}) %reduce-scatter.34.cloned.1.call-update) | async-done | bytes 57360 | tf_op jit(solution)/shard_map/reduce_scatter | solution.py:63
  1387.0 23.6 %all-gather.7 = bf16[1792,128]{1,0:T(8,128)(2,1)S(1)} all-gather(bf16[112,128]{1,0:T(8,128)(2,1)S(1)} %fusion.61), channel_id=9, replica_groups=mesh['leaf'=16,'col'=16] {'leaf'}, dimensions={0}, use_global_device_ids=true | all-gather | bytes 487424 | tf_op jit(solution)/shard_map/all_gather | solution.py:92
  1410.6 1.3 gather_fusion.6
  1411.9 1.3 gather_fusion.7
  1416.5 105.9 %all-reduce.15.cloned.1.call-done = bf16[2,512,128]{2,1,0:T(8,128)(2,1)} async-done(((bf16[2,512,128]{2,1,0:T(8,128)(2,1)}), bf16[2,512,128]{2,1,0:T(8,128)(2,1)}) %all-reduce.15.cloned.1.call-update) | async-done | bytes 262160 | tf_op jit(solution)/shard_map/psum | solution.py:155
  1523.3 1.3 convolution_bitcast_fusion.3
  1524.7 1.3 copy.101
  1526.0 58.5 %reduce-scatter.36.cloned.1.call-done = f32[112,128]{1,0:T(8,128)} async-done(((f32[1792,128]{1,0:T(8,128)}), f32[112,128]{1,0:T(8,128)}) %reduce-scatter.36.cloned.1.call-update) | async-done | bytes 57360 | tf_op jit(solution)/shard_map/reduce_scatter | solution.py:63
  (192 shorter events, 45.5 us)
Async XLA Ops:
  6.5 26.0 %copy-start = (bf16[1,4,112,512]{3,2,1,0:T(8,128)(2,1)S(1)}, bf16[1,4,112,512]{3,2,1,0:T(8,128)(2,1)}, u32[]{:S(2)}) copy-start(bf16[1,4,112,512]{3,2,1,0:T(8,128)(2,1)} %param.38) | copy-start | bytes 1376260
  6.5 121.2 %all-gather.13.cloned.1.call-start = ((), (), s32[]{:S(2)}) async-start(), calls=%async_computation.13 | async-start | bytes 17825792 | tf_op jit(solution)/shard_map/all_gather | solution.py:28
  31.9 0.6 copy-start.12
  32.5 115.4 %copy-start.10 = (bf16[1,4,112,512]{3,2,1,0:T(8,128)(2,1)S(1)}, bf16[1,4,112,512]{3,2,1,0:T(8,128)(2,1)}, u32[]{:S(2)}) copy-start(bf16[1,4,112,512]{3,2,1,0:T(8,128)(2,1)} %param.39) | copy-start | bytes 1376260
  32.5 192.0 %copy-start.17 = (bf16[1,2,112,128]{3,2,1,0:T(8,128)(2,1)S(1)}, bf16[1,2,112,128]{3,2,1,0:T(8,128)(2,1)}, u32[]{:S(2)}) copy-start(bf16[1,2,112,128]{3,2,1,0:T(8,128)(2,1)} %param.35) | copy-start | bytes 172036
  32.8 211.4 %copy-start.1 = (bf16[1,112,1792]{2,1,0:T(8,128)(2,1)S(1)}, bf16[1,112,1792]{2,1,0:T(8,128)(2,1)}, u32[]{:S(2)}) copy-start(bf16[1,112,1792]{2,1,0:T(8,128)(2,1)} %param.37) | copy-start | bytes 1204228
  34.2 190.3 %reduce-scatter.38.cloned.1.call-start = ((), (), s32[]{:S(2)}) async-start(), calls=%async_computation.22 | async-start | bytes 974848
  127.8 117.7 %copy-start.16 = (s32[1,2,4,512]{3,2,1,0:T(4,128)S(1)}, s32[1,2,4,512]{3,2,1,0:T(4,128)}, u32[]{:S(2)}) copy-start(s32[1,2,4,512]{3,2,1,0:T(4,128)} %param.41) | copy-start | bytes 49156
  127.8 117.7 %copy-start.18 = (s32[2]{0:T(128)S(1)}, s32[2]{0:T(128)}, u32[]{:S(2)}) copy-start(s32[2]{0:T(128)} %constant.216) | copy-start | bytes 28
  127.8 117.8 %copy-start.19 = (s32[2]{0:T(128)S(1)}, s32[2]{0:T(128)}, u32[]{:S(2)}) copy-start(s32[2]{0:T(128)} %constant.225) | copy-start | bytes 28
  147.1 285.1 %copy-start.20 = (s32[2]{0:T(128)S(1)}, s32[2]{0:T(128)}, u32[]{:S(2)}) copy-start(s32[2]{0:T(128)} %constant.231) | copy-start | bytes 28
  147.1 171.3 %all-gather.15.cloned.1.call-start = ((), (), s32[]{:S(2)}) async-start(), calls=%async_computation.14 | async-start | bytes 13369344 | tf_op jit(solution)/shard_map/all_gather | solution.py:28
  224.5 186.4 %copy-start.14 = (f32[1,112,128]{2,1,0:T(8,128)S(1)}, f32[1,112,128]{2,1,0:T(8,128)}, u32[]{:S(2)}) copy-start(f32[1,112,128]{2,1,0:T(8,128)} %reduce-scatter.38.cloned.1.call-done) | copy-start | bytes 172036
  244.4 1.0 copy-start.6
  245.4 165.6 %reduce-scatter.40.cloned.1.call-start = ((), (), s32[]{:S(2)}) async-start(), calls=%async_computation.23 | async-start | bytes 974848
  333.6 151.6 %all-gather.17.cloned.1.call-start = ((), (), s32[]{:S(2)}) async-start(), calls=%async_computation.15 | async-start | bytes 8912896 | tf_op jit(solution)/shard_map/all_gather | solution.py:28
  431.2 0.8 copy-start.7
  432.1 141.5 %reduce-scatter.42.cloned.1.call-start = ((), (), s32[]{:S(2)}) async-start(), calls=%async_computation.24 | async-start | bytes 974848
  496.2 137.1 %all-gather.19.cloned.1.call-start = ((), (), s32[]{:S(2)}) async-start(), calls=%async_computation.16 | async-start | bytes 4456448 | tf_op jit(solution)/shard_map/all_gather | solution.py:28
  573.6 143.9 %copy-start.15 = (f32[1,112,128]{2,1,0:T(8,128)S(1)}, f32[1,112,128]{2,1,0:T(8,128)}, u32[]{:S(2)}) copy-start(f32[1,112,128]{2,1,0:T(8,128)} %reduce-scatter.42.cloned.1.call-done) | copy-start | bytes 172036
  593.4 0.7 copy-start.9
  594.1 123.4 %reduce-scatter.44.cloned.1.call-start = ((), (), s32[]{:S(2)}) async-start(), calls=%async_computation.25 | async-start | bytes 974848
  640.1 153.3 %reduce-scatter.28.cloned.1.call-start = ((), (), s32[]{:S(2)}) async-start(), calls=%async_computation.17 | async-start | bytes 974848 | tf_op jit(solution)/shard_map/reduce_scatter | solution.py:63
  737.2 192.7 %copy-start.11 = (bf16[112,128]{1,0:T(8,128)(2,1)}, bf16[112,128]{1,0:T(8,128)(2,1)S(1)}, u32[]{:S(2)}) copy-start(bf16[112,128]{1,0:T(8,128)(2,1)S(1)} %get-tuple-element.233) | copy-start | bytes 86020
  737.3 1.0 copy-start.2
  738.3 190.4 %all-reduce.9.cloned.1.call-start = ((), (), s32[]{:S(2)}) async-start(), calls=%async_computation.9 | async-start | bytes 524288 | tf_op jit(solution)/shard_map/psum | solution.py:155
  821.5 168.0 %reduce-scatter.30.cloned.1.call-start = ((), (), s32[]{:S(2)}) async-start(), calls=%async_computation.18 | async-start | bytes 974848 | tf_op jit(solution)/shard_map/reduce_scatter | solution.py:63
  929.9 593.5 %copy-start.8 = (bf16[1,112,1792]{2,1,0:T(8,128)(2,1)S(1)}, bf16[1,112,1792]{2,1,0:T(8,128)(2,1)}, u32[]{:S(2)}) copy-start(bf16[1,112,1792]{2,1,0:T(8,128)(2,1)} %param.36) | copy-start | bytes 1204228
  930.0 1.0 copy-start.3
  930.9 195.2 %all-reduce.11.cloned.1.call-start = ((), (), s32[]{:S(2)}) async-start(), calls=%async_computation.10 | async-start | bytes 524288 | tf_op jit(solution)/shard_map/psum | solution.py:155
  990.5 23.6 %copy-start.13 = (bf16[112,128]{1,0:T(8,128)(2,1)}, bf16[112,128]{1,0:T(8,128)(2,1)S(1)}, u32[]{:S(2)}) copy-start(bf16[112,128]{1,0:T(8,128)(2,1)S(1)} %fusion.59) | copy-start | bytes 86020
  1019.0 169.2 %reduce-scatter.32.cloned.1.call-start = ((), (), s32[]{:S(2)}) async-start(), calls=%async_computation.19 | async-start | bytes 974848 | tf_op jit(solution)/shard_map/reduce_scatter | solution.py:63
  1128.5 1.0 copy-start.4
  1129.5 195.0 %all-reduce.13.cloned.1.call-start = ((), (), s32[]{:S(2)}) async-start(), calls=%async_computation.11 | async-start | bytes 524288 | tf_op jit(solution)/shard_map/psum | solution.py:155
  1217.5 168.6 %reduce-scatter.34.cloned.1.call-start = ((), (), s32[]{:S(2)}) async-start(), calls=%async_computation.20 | async-start | bytes 974848 | tf_op jit(solution)/shard_map/reduce_scatter | solution.py:63
  1325.4 1.0 copy-start.5
  1326.4 196.0 %all-reduce.15.cloned.1.call-start = ((), (), s32[]{:S(2)}) async-start(), calls=%async_computation.12 | async-start | bytes 524288 | tf_op jit(solution)/shard_map/psum | solution.py:155
  1415.5 169.0 %reduce-scatter.36.cloned.1.call-start = ((), (), s32[]{:S(2)}) async-start(), calls=%async_computation.21 | async-start | bytes 974848 | tf_op jit(solution)/shard_map/reduce_scatter | solution.py:63
Sparse Core Ops, SparseCore 0:
  34.3 93.4 all-gather.12
  147.3 77.2 reduce-scatter.37
  245.5 72.8 all-gather.14
  333.7 77.2 reduce-scatter.39
  432.2 52.9 all-gather.16
  496.3 77.2 reduce-scatter.41
  594.2 38.9 all-gather.18
  640.2 77.2 reduce-scatter.43
  738.4 54.9 reduce-scatter.27
  821.6 106.9 all-reduce.8
  931.2 58.3 reduce-scatter.29
  1019.1 106.9 all-reduce.10
  1129.6 58.5 reduce-scatter.31
  1217.6 106.8 all-reduce.12
  1326.9 59.1 reduce-scatter.33
  1415.6 106.7 all-reduce.14
  1526.1 58.3 reduce-scatter.35
